TPU v7x, 512 devices: a whole 4x4x16 slice. The times are simulated.
512 devices in a mesh: dp: 32 (over y_lo, z), gx: 2 (over core), gy: 8 (over x, y_hi).
Axes of the slice: x: 4, y: 4 (y_hi: 2, y_lo: 2; y = y_hi * 2 + y_lo), z: 16, core: 2. Of those that a mesh axis runs over, the one named last changes fastest.
Arguments:
- field: float32 [32, 64, 1024], P('dp', 'gx', 'gy'), may hold values from -6 to 6
- cotangent: float32 [32, 64, 1024], P('dp', 'gx', 'gy')
- checker: int32 [64, 1024], P('gx', 'gy'), may hold values from 0 to 1, as said below
- weight_in: float32 [3, 3, 32], replicated, may hold values from -2 to 2
- weight_mid: bfloat16 [3, 3, 32, 32], replicated, may hold values from -0.375 to 0.375
- weight_head: bfloat16 [2, 32], replicated, may hold values from -1 to 1
- prior_grads: float32 [32, 2, 8, 23, 9568], P('dp', 'gx', 'gy')
Outputs:
- coupled: float32 [32, 64, 1024], P('dp', 'gx', 'gy')
- field_grad: float32 [32, 64, 1024], P('dp', 'gx', 'gy')
- summed_grads: float32 [24, 9568], replicated
Inputs may be any that keep to these rules, and one draw needn't show every extreme that they name: Each row alternates along the columns: checker[i, j] = (j + p[i]) mod 2, with a parity p[i] of its own for every row i.
All inputs are finite; a program needn't handle non-finite values.
Results may differ from a plain program's by a relative error of at most 0.0034.
Values may be sent and summed in bfloat16 or wider, within the bound.
A program may use at most 64 MiB of HBM per device.

v0:
```python
import math
import jax
import jax.numpy as jnp
from jax import lax
from jax.sharding import PartitionSpec as P


def extended(value, sides, width):
    for axis, dim in sides:
        size, length = (lax.axis_size(axis), value.shape[dim])
        up = [(i, (i + 1) % size) for i in range(size)]
        down = [(j, i) for i, j in up]
        last = lax.slice_in_dim(value, length - width, length, axis=dim)
        initial = lax.slice_in_dim(value, 0, width, axis=dim)
        before = lax.ppermute(last, axis, up)
        after = lax.ppermute(initial, axis, down)
        value = jnp.concatenate([before, value, after], axis=dim)
    return value


def first_conv(padded, weight_in, row_count, col_count):
    total = jnp.zeros((weight_in.shape[2], row_count, col_count), jnp.float32)
    for row_tap in range(3):
        for col_tap in range(3):
            window = padded[row_tap : row_tap + row_count, col_tap : col_tap + col_count]
            total = total + weight_in[row_tap, col_tap][:, None, None] * window[None]
    return total


def on_device(field, cotangent, checker, weight_in, weight_mid, weight_head, prior_grads):
    highest = lax.Precision.HIGHEST
    row_count = field.shape[1]
    col_count = field.shape[2]
    hidden_width = weight_mid.shape[2]
    cell_total = (
        lax.axis_size("dp") * row_count * lax.axis_size("gx") * col_count * lax.axis_size("gy")
    )
    grad_scale = 1.0 / math.sqrt(cell_total)
    values = field[0]
    downstream = cotangent[0]
    frozen = checker.astype(jnp.float32)
    unfrozen = 1.0 - frozen
    masked = frozen * values
    partial_prior = prior_grads.reshape(prior_grads.shape[3], prior_grads.shape[4])
    padded_field = extended(masked, (("gx", 0), ("gy", 1)), 1)
    hidden_one = jnp.tanh(first_conv(padded_field, weight_in, row_count, col_count)).astype(
        jnp.bfloat16
    )
    hidden_pad = extended(hidden_one, (("gx", 1), ("gy", 2)), 1)
    hidden_inner = hidden_pad[:, 1:-1, 1:-1]
    pre_two = jnp.zeros((hidden_width, row_count, col_count), jnp.float32)
    for row_tap in range(3):
        for col_tap in range(3):
            window = hidden_pad[:, row_tap : row_tap + row_count, col_tap : col_tap + col_count]
            pre_two = pre_two + jnp.einsum(
                "oc,cxy->oxy",
                weight_mid[row_tap, col_tap],
                window,
                preferred_element_type=jnp.float32,
            )
    hidden_two = jnp.tanh(pre_two).astype(jnp.bfloat16)
    pair = jnp.einsum("ko,oxy->kxy", weight_head, hidden_two, preferred_element_type=jnp.float32)
    expo = jnp.exp(pair[0])
    coupled = masked + unfrozen * (values * expo + pair[1])
    d_pair = jnp.stack([unfrozen * downstream * values * expo, unfrozen * downstream]).astype(
        jnp.bfloat16
    )
    grad_head = jnp.einsum("kxy,oxy->ko", d_pair, hidden_two, preferred_element_type=jnp.float32)
    d_hidden_two = jnp.einsum(
        "ko,kxy->oxy", weight_head, d_pair, preferred_element_type=jnp.float32
    )
    two_f = hidden_two.astype(jnp.float32)
    d_pre_two = (d_hidden_two * (1.0 - two_f * two_f)).astype(jnp.bfloat16)
    d_two_pad = extended(d_pre_two, (("gx", 1), ("gy", 2)), 1)
    mid_list = []
    d_hidden_one = jnp.zeros((hidden_width, row_count, col_count), jnp.float32)
    for row_tap in range(3):
        for col_tap in range(3):
            window = hidden_pad[:, row_tap : row_tap + row_count, col_tap : col_tap + col_count]
            mid_list.append(
                jnp.einsum("oxy,cxy->oc", d_pre_two, window, preferred_element_type=jnp.float32)
            )
            back_window = d_two_pad[
                :, 2 - row_tap : 2 - row_tap + row_count, 2 - col_tap : 2 - col_tap + col_count
            ]
            d_hidden_one = d_hidden_one + jnp.einsum(
                "oc,oxy->cxy",
                weight_mid[row_tap, col_tap],
                back_window,
                preferred_element_type=jnp.float32,
            )
    one_f = hidden_inner.astype(jnp.float32)
    d_pre_one = d_hidden_one * (1.0 - one_f * one_f)
    in_list = []
    for row_tap in range(3):
        for col_tap in range(3):
            window = padded_field[row_tap : row_tap + row_count, col_tap : col_tap + col_count]
            in_list.append(jnp.einsum("oxy,xy->o", d_pre_one, window, precision=highest))
    d_one_pad = extended(d_pre_one, (("gx", 1), ("gy", 2)), 1)
    d_masked = jnp.zeros((row_count, col_count), jnp.float32)
    for row_tap in range(3):
        for col_tap in range(3):
            back_window = d_one_pad[
                :, 2 - row_tap : 2 - row_tap + row_count, 2 - col_tap : 2 - col_tap + col_count
            ]
            d_masked = d_masked + jnp.einsum(
                "o,oxy->xy", weight_in[row_tap, col_tap], back_window, precision=highest
            )
    field_grad = frozen * downstream + unfrozen * downstream * expo + frozen * d_masked
    layer_grads = (
        jnp.concatenate(
            [jnp.stack(in_list).reshape(-1), jnp.stack(mid_list).reshape(-1), grad_head.reshape(-1)]
        )
        * grad_scale
    )
    stacked = jnp.concatenate([layer_grads[None], partial_prior], axis=0)
    summed_grads = lax.psum(stacked, ("dp", "gx", "gy"))
    return (coupled[None], field_grad[None], summed_grads)


def solution(mesh):
    placed = (
        P("dp", "gx", "gy"),
        P("dp", "gx", "gy"),
        P("gx", "gy"),
        P(),
        P(),
        P(),
        P("dp", "gx", "gy", None, None),
    )
    return jax.shard_map(
        on_device,
        mesh=mesh,
        in_specs=placed,
        out_specs=(P("dp", "gx", "gy"), P("dp", "gx", "gy"), P()),
        check_vma=False,
    )
```

profile of v0, /device:TPU:1, one launch (start us, length us, event | category | flops | bytes accessed | tf_op | source)
XLA Modules:
  0.0 572.6 jit_solution(7181842597088774773)
XLA Ops:
  7.2 0.7 bitcast_multiply_fusion.6
  8.0 8.8 %collective-permute-start = (f32[1,128]{1,0:T(1,128)S(1)}, f32[1,128]{1,0:T(1,128)S(1)}, u32[]{:S(2)}, u32[]{:S(2)}) collective-permute-start(f32[1,128]{1,0:T(1,128)S(1)} %get-tuple-element.38), channel_id=1, source_target_pairs={{0,8},{8,0},{1,9},{9,1},{2,10},{10,2},{3,11},{11,3},{4,12},{12,4},... | collective-permute-start | bytes 1544 | tf_op jit(solution)/shard_map/ppermute | solution.py:15
  16.8 1.9 collective-permute-start.1
  18.7 0.8 slice_bitcast_fusion.8
  19.6 1.3 copy.81
  20.9 1.9 collective-permute-start.2
  22.9 7.0 %collective-permute-start.3 = (f32[34,1]{1,0:T(8,128)S(1)}, f32[34,1]{1,0:T(8,128)S(1)}, u32[]{:S(2)}, u32[]{:S(2)}) collective-permute-start(f32[34,1]{1,0:T(8,128)S(1)} %get-tuple-element.33), channel_id=1, source_target_pairs={{1,0},{2,1},{3,2},{4,3},{5,4},{6,5},{7,6},{0,7},{9,8},{10,9},{11,1... | collective-permute-start | bytes 416 | tf_op jit(solution)/shard_map/ppermute | solution.py:16
  29.9 0.9 collective-permute-done.3
  31.3 3.5 collective-permute-start.4
  34.9 1.9 collective-permute-start.5
  37.0 0.9 collective-permute-done.5
  38.1 1.9 collective-permute-start.6
  40.0 7.5 %collective-permute-start.7 = (bf16[32,34,1]{2,0,1:T(8,128)(2,1)S(1)}, bf16[32,34,1]{2,0,1:T(8,128)(2,1)S(1)}, u32[]{:S(2)}, u32[]{:S(2)}) collective-permute-start(bf16[32,34,1]{2,0,1:T(8,128)(2,1)S(1)} %get-tuple-element.16), channel_id=1, source_target_pairs={{1,0},{2,1},{3,2},{4,3},{5,4},{6,5},{7,6},{0,7},{9,8},{10,9},{11,1... | collective-permute-start | bytes 6536 | tf_op jit(solution)/shard_map/ppermute | solution.py:16
  48.0 4.6 collective-permute-done.6
  52.7 4.9 collective-permute-done.7
  60.0 0.6 fusion.96
  63.3 2.9 collective-permute-start.9
  66.1 1.9 collective-permute-start.8
  68.5 0.7 collective-permute-done.8
  69.4 5.6 collective-permute-start.10
  75.0 1.9 collective-permute-start.11
  77.5 3.5 collective-permute-done.10
  81.0 7.4 %collective-permute-done.11 = bf16[32,34,1]{2,0,1:T(8,128)(2,1)S(1)} collective-permute-done((bf16[32,34,1]{2,0,1:T(8,128)(2,1)S(1)}, bf16[32,34,1]{2,0,1:T(8,128)(2,1)S(1)}, u32[]{:S(2)}, u32[]{:S(2)}) %collective-permute-start.11) | collective-permute-done | bytes 2208 | tf_op jit(solution)/shard_map/ppermute | solution.py:15
  95.8 3.2 collective-permute-start.13
  99.0 1.9 collective-permute-start.12
  100.9 1.0 pad_maximum_fusion.1
  103.1 6.0 %collective-permute-start.14 = (f32[32,34,1]{1,0,2:T(8,128)S(1)}, f32[32,34,1]{1,0,2:T(8,128)S(1)}, u32[]{:S(2)}, u32[]{:S(2)}) collective-permute-start(f32[32,34,1]{1,0,2:T(8,128)S(1)} %copy.33), channel_id=1, source_target_pairs={{1,0},{2,1},{3,2},{4,3},{5,4},{6,5},{7,6},{0,7},{9,8},{10,9},{11,1... | collective-permute-start | bytes 13064 | tf_op jit(solution)/shard_map/ppermute | solution.py:16
  109.5 1.9 collective-permute-start.15
  112.8 4.7 collective-permute-done.15
  121.3 0.6 fusion.86
  121.9 441.7 %all-reduce.2.cloned.1.call-done = f32[24,9568]{1,0:T(8,128)} async-done(((f32[24,9568]{1,0:T(8,128)}), f32[24,9568]{1,0:T(8,128)}) %all-reduce.2.cloned.1.call-update) | async-done | bytes 918544 | tf_op jit(solution)/shard_map/psum | solution.py:117
  563.6 2.2 copy.91
  (101 shorter events, 21.6 us)
Async XLA Ops:
  7.2 52.4 %copy-start = (bf16[2,32]{1,0:T(2,128)(2,1)S(1)}, bf16[2,32]{1,0:T(2,128)(2,1)}, u32[]{:S(2)}) copy-start(bf16[2,32]{1,0:T(2,128)(2,1)} %param.12) | copy-start | bytes 388
  7.2 556.4 %all-reduce.2.cloned.1.call-start = ((), (), s32[]{:S(2)}) async-start(), calls=%async_computation | async-start | bytes 1843200 | tf_op jit(solution)/shard_map/psum | solution.py:117
  8.0 12.9 %collective-permute-start = (f32[1,128]{1,0:T(1,128)S(1)}, f32[1,128]{1,0:T(1,128)S(1)}, u32[]{:S(2)}, u32[]{:S(2)}) collective-permute-start(f32[1,128]{1,0:T(1,128)S(1)} %get-tuple-element.38), channel_id=1, source_target_pairs={{0,8},{8,0},{1,9},{9,1},{2,10},{10,2},{3,11},{11,3},{4,12},{12,4},... | collective-permute-start | bytes 1544 | tf_op jit(solution)/shard_map/ppermute | solution.py:15
  16.8 4.1 collective-permute-start.1
  19.5 17.2 %copy-start.1 = (bf16[3,3,32,32]{3,2,1,0:T(8,128)(2,1)S(1)}, bf16[3,3,32,32]{3,2,1,0:T(8,128)(2,1)}, u32[]{:S(2)}) copy-start(bf16[3,3,32,32]{3,2,1,0:T(8,128)(2,1)} %param.11) | copy-start | bytes 55300
  20.9 8.9 %collective-permute-start.2 = (f32[34,1]{1,0:T(8,128)S(1)}, f32[34,1]{1,0:T(8,128)S(1)}, u32[]{:S(2)}, u32[]{:S(2)}) collective-permute-start(f32[34,1]{1,0:T(8,128)S(1)} %get-tuple-element.32), channel_id=1, source_target_pairs={{0,1},{1,2},{2,3},{3,4},{4,5},{5,6},{6,7},{7,0},{8,9},{9,10},{10,1... | collective-permute-start | bytes 416 | tf_op jit(solution)/shard_map/ppermute | solution.py:15
  22.9 7.9 %collective-permute-start.3 = (f32[34,1]{1,0:T(8,128)S(1)}, f32[34,1]{1,0:T(8,128)S(1)}, u32[]{:S(2)}, u32[]{:S(2)}) collective-permute-start(f32[34,1]{1,0:T(8,128)S(1)} %get-tuple-element.33), channel_id=1, source_target_pairs={{1,0},{2,1},{3,2},{4,3},{5,4},{6,5},{7,6},{0,7},{9,8},{10,9},{11,1... | collective-permute-start | bytes 416 | tf_op jit(solution)/shard_map/ppermute | solution.py:16
  31.3 5.7 collective-permute-start.4
  34.9 3.1 collective-permute-start.5
  38.1 14.5 %collective-permute-start.6 = (bf16[32,34,1]{2,0,1:T(8,128)(2,1)S(1)}, bf16[32,34,1]{2,0,1:T(8,128)(2,1)S(1)}, u32[]{:S(2)}, u32[]{:S(2)}) collective-permute-start(bf16[32,34,1]{2,0,1:T(8,128)(2,1)S(1)} %get-tuple-element.15), channel_id=1, source_target_pairs={{0,1},{1,2},{2,3},{3,4},{4,5},{5,6},{6,7},{7,0},{8,9},{9,10},{10,1... | collective-permute-start | bytes 6536 | tf_op jit(solution)/shard_map/ppermute | solution.py:15
  40.0 17.5 %collective-permute-start.7 = (bf16[32,34,1]{2,0,1:T(8,128)(2,1)S(1)}, bf16[32,34,1]{2,0,1:T(8,128)(2,1)S(1)}, u32[]{:S(2)}, u32[]{:S(2)}) collective-permute-start(bf16[32,34,1]{2,0,1:T(8,128)(2,1)S(1)} %get-tuple-element.16), channel_id=1, source_target_pairs={{1,0},{2,1},{3,2},{4,3},{5,4},{6,5},{7,6},{0,7},{9,8},{10,9},{11,1... | collective-permute-start | bytes 6536 | tf_op jit(solution)/shard_map/ppermute | solution.py:16
  59.2 0.7 copy-start.2
  59.2 0.7 copy-start.4
  59.2 0.7 copy-start.5
  63.3 5.2 collective-permute-start.9
  66.1 3.1 collective-permute-start.8
  69.4 11.6 %collective-permute-start.10 = (bf16[32,34,1]{2,0,1:T(8,128)(2,1)S(1)}, bf16[32,34,1]{2,0,1:T(8,128)(2,1)S(1)}, u32[]{:S(2)}, u32[]{:S(2)}) collective-permute-start(bf16[32,34,1]{2,0,1:T(8,128)(2,1)S(1)} %get-tuple-element.11), channel_id=1, source_target_pairs={{1,0},{2,1},{3,2},{4,3},{5,4},{6,5},{7,6},{0,7},{9,8},{10,9},{11,1... | collective-permute-start | bytes 6536 | tf_op jit(solution)/shard_map/ppermute | solution.py:16
  75.0 13.3 %collective-permute-start.11 = (bf16[32,34,1]{2,0,1:T(8,128)(2,1)S(1)}, bf16[32,34,1]{2,0,1:T(8,128)(2,1)S(1)}, u32[]{:S(2)}, u32[]{:S(2)}) collective-permute-start(bf16[32,34,1]{2,0,1:T(8,128)(2,1)S(1)} %get-tuple-element.12), channel_id=1, source_target_pairs={{0,1},{1,2},{2,3},{3,4},{4,5},{5,6},{6,7},{7,0},{8,9},{9,10},{10,1... | collective-permute-start | bytes 6536 | tf_op jit(solution)/shard_map/ppermute | solution.py:15
  95.4 6.6 %copy-start.3 = (f32[3,3,32]{2,1,0:T(4,128)S(1)}, f32[3,3,32]{2,1,0:T(4,128)}, u32[]{:S(2)}) copy-start(f32[3,3,32]{2,1,0:T(4,128)} %param.10) | copy-start | bytes 3460
  95.8 6.6 %collective-permute-start.13 = (f32[32,1,128]{2,0,1:T(8,128)S(1)}, f32[32,1,128]{2,0,1:T(8,128)S(1)}, u32[]{:S(2)}, u32[]{:S(2)}) collective-permute-start(f32[32,1,128]{2,0,1:T(8,128)S(1)} %get-tuple-element.8), channel_id=1, source_target_pairs={{8,0},{0,8},{9,1},{1,9},{10,2},{2,10},{11,3},{3,11},{12,4},{4,12},... | collective-permute-start | bytes 49160 | tf_op jit(solution)/shard_map/ppermute | solution.py:16
  99.0 3.4 collective-permute-start.12
  103.1 9.1 %collective-permute-start.14 = (f32[32,34,1]{1,0,2:T(8,128)S(1)}, f32[32,34,1]{1,0,2:T(8,128)S(1)}, u32[]{:S(2)}, u32[]{:S(2)}) collective-permute-start(f32[32,34,1]{1,0,2:T(8,128)S(1)} %copy.33), channel_id=1, source_target_pairs={{1,0},{2,1},{3,2},{4,3},{5,4},{6,5},{7,6},{0,7},{9,8},{10,9},{11,1... | collective-permute-start | bytes 13064 | tf_op jit(solution)/shard_map/ppermute | solution.py:16
  109.5 8.1 %collective-permute-start.15 = (f32[32,34,1]{1,0,2:T(8,128)S(1)}, f32[32,34,1]{1,0,2:T(8,128)S(1)}, u32[]{:S(2)}, u32[]{:S(2)}) collective-permute-start(f32[32,34,1]{1,0,2:T(8,128)S(1)} %copy.35), channel_id=1, source_target_pairs={{0,1},{1,2},{2,3},{3,4},{4,5},{5,6},{6,7},{7,0},{8,9},{9,10},{10,1... | collective-permute-start | bytes 13064 | tf_op jit(solution)/shard_map/ppermute | solution.py:15
Sparse Core Ops, SparseCore 0:
  102.5 461.0 all-reduce.1
where the time goes:
time: 573 us
  waiting for transfers between devices  469 us (82%)
  starting transfers between devices  59.9 us (10%)
  matrix products  16.1 us (3%)
  between operations  14.6 us (3%)
  local copies, waits for them, and re-layouts  7.8 us (1%)
    psum x1, waiting for transfers between devices, on_device(): summed_grads = lax.psum(stacked, ('dp', 'gx', 'gy'))  442 us
    ppermute x8, starting transfers between devices, extended(): after = lax.ppermute(initial, axis, down)  36 us
    ppermute x8, starting transfers between devices, extended(): before = lax.ppermute(last, axis, up)  23.8 us
    ppermute x8, waiting for transfers between devices, extended(): before = lax.ppermute(last, axis, up)  17.5 us
  transfers between devices with their start and end apart: 17, of which 9 were waited for; matrix products, arithmetic and copies ran while one was open for 2% of the time, Pallas kernels for 0%

commit v1 on v0

--- a/solution.py
+++ b/solution.py
@@ -3,6 +3,7 @@
 import jax.numpy as jnp
 from jax import lax
 from jax.sharding import PartitionSpec as P
+from jax.lax import psum
 
 
 def extended(value, sides, width):
@@ -114,7 +115,7 @@
         * grad_scale
     )
     stacked = jnp.concatenate([layer_grads[None], partial_prior], axis=0)
-    summed_grads = lax.psum(stacked, ("dp", "gx", "gy"))
+    summed_grads = psum(psum(stacked, axis_name="dp"), axis_name=("gx", "gy"))
     return (coupled[None], field_grad[None], summed_grads)
 
 

time: 573 us -> 527 us (0.920)
  waiting for transfers between devices: 469 us -> 422 us
    psum x1 -> x2, waiting for transfers between devices: 442 us -> 394 us  [on_device(): summed_grads = psum(psum(stacked, axis_name='dp'), axis_name=('gx', 'gy'))]
  transfers between devices with their start and end apart: 17 -> 18, of which waited for: 9 -> 10; matrix products, arithmetic and copies ran while one was open for 2% -> 3% of each run, Pallas kernels for 0% -> 0%
where the time goes in v1:
time: 527 us
  waiting for transfers between devices  422 us (80%)
  starting transfers between devices  59.9 us (11%)
  matrix products  16.2 us (3%)
  between operations  14.6 us (3%)
  local copies, waits for them, and re-layouts  8.54 us (2%)
  other arithmetic  5.95 us (1%)
    psum x2, waiting for transfers between devices, on_device(): summed_grads = psum(psum(stacked, axis_name='dp'), axis_name=('gx', 'gy'))  394 us
    ppermute x8, starting transfers between devices, extended(): after = lax.ppermute(initial, axis, down)  35.8 us
    ppermute x8, starting transfers between devices, extended(): before = lax.ppermute(last, axis, up)  23.8 us
    ppermute x8, waiting for transfers between devices, extended(): before = lax.ppermute(last, axis, up)  17.5 us
  transfers between devices with their start and end apart: 18, of which 10 were waited for; matrix products, arithmetic and copies ran while one was open for 3% of the time, Pallas kernels for 0%

profile of v1, /device:TPU:1, one launch (start us, length us, event | category | flops | bytes accessed | tf_op | source)
XLA Modules:
  0.0 526.7 jit_solution(14420198657777059344)
XLA Ops:
  7.2 0.7 bitcast_multiply_fusion.6
  8.0 8.8 %collective-permute-start = (f32[1,128]{1,0:T(1,128)S(1)}, f32[1,128]{1,0:T(1,128)S(1)}, u32[]{:S(2)}, u32[]{:S(2)}) collective-permute-start(f32[1,128]{1,0:T(1,128)S(1)} %get-tuple-element.38), channel_id=1, source_target_pairs={{0,8},{8,0},{1,9},{9,1},{2,10},{10,2},{3,11},{11,3},{4,12},{12,4},... | collective-permute-start | bytes 1544 | tf_op jit(solution)/shard_map/ppermute | solution.py:16
  16.8 1.9 collective-permute-start.1
  18.7 0.8 slice_bitcast_fusion.8
  19.6 1.3 copy.81
  20.9 1.9 collective-permute-start.2
  22.9 7.0 %collective-permute-start.3 = (f32[34,1]{1,0:T(8,128)S(1)}, f32[34,1]{1,0:T(8,128)S(1)}, u32[]{:S(2)}, u32[]{:S(2)}) collective-permute-start(f32[34,1]{1,0:T(8,128)S(1)} %get-tuple-element.33), channel_id=1, source_target_pairs={{1,0},{2,1},{3,2},{4,3},{5,4},{6,5},{7,6},{0,7},{9,8},{10,9},{11,1... | collective-permute-start | bytes 416 | tf_op jit(solution)/shard_map/ppermute | solution.py:17
  29.9 0.9 collective-permute-done.3
  31.3 3.5 collective-permute-start.4
  34.9 1.9 collective-permute-start.5
  37.0 0.9 collective-permute-done.5
  38.1 1.9 collective-permute-start.6
  40.0 7.5 %collective-permute-start.7 = (bf16[32,34,1]{2,0,1:T(8,128)(2,1)S(1)}, bf16[32,34,1]{2,0,1:T(8,128)(2,1)S(1)}, u32[]{:S(2)}, u32[]{:S(2)}) collective-permute-start(bf16[32,34,1]{2,0,1:T(8,128)(2,1)S(1)} %get-tuple-element.16), channel_id=1, source_target_pairs={{1,0},{2,1},{3,2},{4,3},{5,4},{6,5},{7,6},{0,7},{9,8},{10,9},{11,1... | collective-permute-start | bytes 6536 | tf_op jit(solution)/shard_map/ppermute | solution.py:17
  48.0 4.6 collective-permute-done.6
  52.7 4.9 collective-permute-done.7
  63.3 2.9 collective-permute-start.9
  66.2 1.9 collective-permute-start.8
  69.4 5.6 %collective-permute-start.10 = (bf16[32,34,1]{2,0,1:T(8,128)(2,1)S(1)}, bf16[32,34,1]{2,0,1:T(8,128)(2,1)S(1)}, u32[]{:S(2)}, u32[]{:S(2)}) collective-permute-start(bf16[32,34,1]{2,0,1:T(8,128)(2,1)S(1)} %get-tuple-element.11), channel_id=1, source_target_pairs={{1,0},{2,1},{3,2},{4,3},{5,4},{6,5},{7,6},{0,7},{9,8},{10,9},{11,1... | collective-permute-start | bytes 6536 | tf_op jit(solution)/shard_map/ppermute | solution.py:17
  75.0 1.9 collective-permute-start.11
  77.5 3.5 collective-permute-done.10
  81.0 7.4 %collective-permute-done.11 = bf16[32,34,1]{2,0,1:T(8,128)(2,1)S(1)} collective-permute-done((bf16[32,34,1]{2,0,1:T(8,128)(2,1)S(1)}, bf16[32,34,1]{2,0,1:T(8,128)(2,1)S(1)}, u32[]{:S(2)}, u32[]{:S(2)}) %collective-permute-start.11) | collective-permute-done | bytes 2208 | tf_op jit(solution)/shard_map/ppermute | solution.py:16
  95.8 3.2 collective-permute-start.13
  99.0 1.9 collective-permute-start.12
  100.9 1.0 pad_maximum_fusion.1
  103.3 5.8 %collective-permute-start.14 = (f32[32,34,1]{1,0,2:T(8,128)S(1)}, f32[32,34,1]{1,0,2:T(8,128)S(1)}, u32[]{:S(2)}, u32[]{:S(2)}) collective-permute-start(f32[32,34,1]{1,0,2:T(8,128)S(1)} %copy.33), channel_id=1, source_target_pairs={{1,0},{2,1},{3,2},{4,3},{5,4},{6,5},{7,6},{0,7},{9,8},{10,9},{11,1... | collective-permute-start | bytes 13064 | tf_op jit(solution)/shard_map/ppermute | solution.py:17
  109.5 1.9 collective-permute-start.15
  112.9 4.7 collective-permute-done.15
  117.6 1.4 copy.36
  119.0 1.4 pad_maximum_fusion
  121.8 214.8 %all-reduce.3.cloned.1.call-done = f32[24,9568]{1,0:T(8,128)} async-done(((f32[24,9568]{1,0:T(8,128)}), f32[24,9568]{1,0:T(8,128)}) %all-reduce.3.cloned.1.call-update) | async-done | bytes 918544 | tf_op jit(solution)/shard_map/psum | solution.py:118
  338.5 179.1 %all-reduce.5.cloned.1.call-done = f32[24,9568]{1,0:T(8,128)} async-done(((f32[24,9568]{1,0:T(8,128)}), f32[24,9568]{1,0:T(8,128)}) %all-reduce.5.cloned.1.call-update) | async-done | bytes 918544 | tf_op jit(solution)/shard_map/psum | solution.py:118
  517.7 2.2 copy.92
  (104 shorter events, 22.8 us)
Async XLA Ops:
  7.2 52.4 %copy-start = (bf16[2,32]{1,0:T(2,128)(2,1)S(1)}, bf16[2,32]{1,0:T(2,128)(2,1)}, u32[]{:S(2)}) copy-start(bf16[2,32]{1,0:T(2,128)(2,1)} %param.12) | copy-start | bytes 388
  7.2 329.4 %all-reduce.3.cloned.1.call-start = ((), (), s32[]{:S(2)}) async-start(), calls=%async_computation | async-start | bytes 1843200 | tf_op jit(solution)/shard_map/psum | solution.py:118
  8.0 12.9 %collective-permute-start = (f32[1,128]{1,0:T(1,128)S(1)}, f32[1,128]{1,0:T(1,128)S(1)}, u32[]{:S(2)}, u32[]{:S(2)}) collective-permute-start(f32[1,128]{1,0:T(1,128)S(1)} %get-tuple-element.38), channel_id=1, source_target_pairs={{0,8},{8,0},{1,9},{9,1},{2,10},{10,2},{3,11},{11,3},{4,12},{12,4},... | collective-permute-start | bytes 1544 | tf_op jit(solution)/shard_map/ppermute | solution.py:16
  16.8 4.1 collective-permute-start.1
  19.5 17.2 %copy-start.1 = (bf16[3,3,32,32]{3,2,1,0:T(8,128)(2,1)S(1)}, bf16[3,3,32,32]{3,2,1,0:T(8,128)(2,1)}, u32[]{:S(2)}) copy-start(bf16[3,3,32,32]{3,2,1,0:T(8,128)(2,1)} %param.11) | copy-start | bytes 55300
  20.9 8.9 %collective-permute-start.2 = (f32[34,1]{1,0:T(8,128)S(1)}, f32[34,1]{1,0:T(8,128)S(1)}, u32[]{:S(2)}, u32[]{:S(2)}) collective-permute-start(f32[34,1]{1,0:T(8,128)S(1)} %get-tuple-element.32), channel_id=1, source_target_pairs={{0,1},{1,2},{2,3},{3,4},{4,5},{5,6},{6,7},{7,0},{8,9},{9,10},{10,1... | collective-permute-start | bytes 416 | tf_op jit(solution)/shard_map/ppermute | solution.py:16
  22.9 7.9 %collective-permute-start.3 = (f32[34,1]{1,0:T(8,128)S(1)}, f32[34,1]{1,0:T(8,128)S(1)}, u32[]{:S(2)}, u32[]{:S(2)}) collective-permute-start(f32[34,1]{1,0:T(8,128)S(1)} %get-tuple-element.33), channel_id=1, source_target_pairs={{1,0},{2,1},{3,2},{4,3},{5,4},{6,5},{7,6},{0,7},{9,8},{10,9},{11,1... | collective-permute-start | bytes 416 | tf_op jit(solution)/shard_map/ppermute | solution.py:17
  31.3 5.7 %collective-permute-start.4 = (bf16[32,1,128]{2,0,1:T(8,128)(2,1)S(1)}, bf16[32,1,128]{2,0,1:T(8,128)(2,1)S(1)}, u32[]{:S(2)}, u32[]{:S(2)}) collective-permute-start(bf16[32,1,128]{2,0,1:T(8,128)(2,1)S(1)} %get-tuple-element.19), channel_id=1, source_target_pairs={{0,8},{8,0},{1,9},{9,1},{2,10},{10,2},{3,11},{11,3},{4,12},{12,4},... | collective-permute-start | bytes 24584 | tf_op jit(solution)/shard_map/ppermute | solution.py:16
  34.9 3.1 collective-permute-start.5
  38.1 14.5 %collective-permute-start.6 = (bf16[32,34,1]{2,0,1:T(8,128)(2,1)S(1)}, bf16[32,34,1]{2,0,1:T(8,128)(2,1)S(1)}, u32[]{:S(2)}, u32[]{:S(2)}) collective-permute-start(bf16[32,34,1]{2,0,1:T(8,128)(2,1)S(1)} %get-tuple-element.15), channel_id=1, source_target_pairs={{0,1},{1,2},{2,3},{3,4},{4,5},{5,6},{6,7},{7,0},{8,9},{9,10},{10,1... | collective-permute-start | bytes 6536 | tf_op jit(solution)/shard_map/ppermute | solution.py:16
  40.0 17.5 %collective-permute-start.7 = (bf16[32,34,1]{2,0,1:T(8,128)(2,1)S(1)}, bf16[32,34,1]{2,0,1:T(8,128)(2,1)S(1)}, u32[]{:S(2)}, u32[]{:S(2)}) collective-permute-start(bf16[32,34,1]{2,0,1:T(8,128)(2,1)S(1)} %get-tuple-element.16), channel_id=1, source_target_pairs={{1,0},{2,1},{3,2},{4,3},{5,4},{6,5},{7,6},{0,7},{9,8},{10,9},{11,1... | collective-permute-start | bytes 6536 | tf_op jit(solution)/shard_map/ppermute | solution.py:17
  59.2 0.7 copy-start.2
  59.2 0.7 copy-start.4
  59.2 0.7 copy-start.5
  63.3 5.2 collective-permute-start.9
  66.2 3.1 collective-permute-start.8
  69.4 11.5 %collective-permute-start.10 = (bf16[32,34,1]{2,0,1:T(8,128)(2,1)S(1)}, bf16[32,34,1]{2,0,1:T(8,128)(2,1)S(1)}, u32[]{:S(2)}, u32[]{:S(2)}) collective-permute-start(bf16[32,34,1]{2,0,1:T(8,128)(2,1)S(1)} %get-tuple-element.11), channel_id=1, source_target_pairs={{1,0},{2,1},{3,2},{4,3},{5,4},{6,5},{7,6},{0,7},{9,8},{10,9},{11,1... | collective-permute-start | bytes 6536 | tf_op jit(solution)/shard_map/ppermute | solution.py:17
  75.0 13.3 %collective-permute-start.11 = (bf16[32,34,1]{2,0,1:T(8,128)(2,1)S(1)}, bf16[32,34,1]{2,0,1:T(8,128)(2,1)S(1)}, u32[]{:S(2)}, u32[]{:S(2)}) collective-permute-start(bf16[32,34,1]{2,0,1:T(8,128)(2,1)S(1)} %get-tuple-element.12), channel_id=1, source_target_pairs={{0,1},{1,2},{2,3},{3,4},{4,5},{5,6},{6,7},{7,0},{8,9},{9,10},{10,1... | collective-permute-start | bytes 6536 | tf_op jit(solution)/shard_map/ppermute | solution.py:16
  95.4 6.6 %copy-start.3 = (f32[3,3,32]{2,1,0:T(4,128)S(1)}, f32[3,3,32]{2,1,0:T(4,128)}, u32[]{:S(2)}) copy-start(f32[3,3,32]{2,1,0:T(4,128)} %param.10) | copy-start | bytes 3460
  95.8 6.8 %collective-permute-start.13 = (f32[32,1,128]{2,0,1:T(8,128)S(1)}, f32[32,1,128]{2,0,1:T(8,128)S(1)}, u32[]{:S(2)}, u32[]{:S(2)}) collective-permute-start(f32[32,1,128]{2,0,1:T(8,128)S(1)} %get-tuple-element.8), channel_id=1, source_target_pairs={{8,0},{0,8},{9,1},{1,9},{10,2},{2,10},{11,3},{3,11},{12,4},{4,12},... | collective-permute-start | bytes 49160 | tf_op jit(solution)/shard_map/ppermute | solution.py:17
  99.0 3.6 collective-permute-start.12
  102.4 415.3 %all-reduce.5.cloned.1.call-start = ((), (), s32[]{:S(2)}) async-start(), calls=%async_computation.1 | async-start | bytes 1843200 | tf_op jit(solution)/shard_map/psum | solution.py:118
  103.3 8.9 %collective-permute-start.14 = (f32[32,34,1]{1,0,2:T(8,128)S(1)}, f32[32,34,1]{1,0,2:T(8,128)S(1)}, u32[]{:S(2)}, u32[]{:S(2)}) collective-permute-start(f32[32,34,1]{1,0,2:T(8,128)S(1)} %copy.33), channel_id=1, source_target_pairs={{1,0},{2,1},{3,2},{4,3},{5,4},{6,5},{7,6},{0,7},{9,8},{10,9},{11,1... | collective-permute-start | bytes 13064 | tf_op jit(solution)/shard_map/ppermute | solution.py:17
  109.5 8.1 %collective-permute-start.15 = (f32[32,34,1]{1,0,2:T(8,128)S(1)}, f32[32,34,1]{1,0,2:T(8,128)S(1)}, u32[]{:S(2)}, u32[]{:S(2)}) collective-permute-start(f32[32,34,1]{1,0,2:T(8,128)S(1)} %copy.35), channel_id=1, source_target_pairs={{0,1},{1,2},{2,3},{3,4},{4,5},{5,6},{6,7},{7,0},{8,9},{9,10},{10,1... | collective-permute-start | bytes 13064 | tf_op jit(solution)/shard_map/ppermute | solution.py:16
Sparse Core Ops, SparseCore 0:
  102.5 234.0 all-reduce.2
  339.8 177.8 all-reduce.4
